TPU v7x, 32 devices: a whole 2x2x4 slice. The times are simulated.
32 devices in a mesh: pipe: 4 (over x, core), dp: 8 (over z, y).
Axes of the slice: x: 2, y: 2, z: 4, core: 2. Of those that a mesh axis runs over, the one named last changes fastest.
Arguments:
- section_input: bfloat16 [4, 2048, 2048], P('pipe', 'dp'), may hold values from -6 to 6
- top_grad: bfloat16 [2048, 2048], P('dp'), may hold values from -6 to 6
- w_in: bfloat16 [4, 2048, 3072], P('pipe', 'dp'), may hold values from -0.125 to 0.125
- w_out: bfloat16 [4, 1024, 2048], P('pipe', 'dp'), may hold values from -0.1875 to 0.1875
- segments: int32 [16, 128], P('dp'), may hold values from 0 to 3, never falling along the last dimension, each value on 1 to 64 neighbouring positions
Outputs:
- section_grads: bfloat16 [4, 2048, 2048], P('pipe', 'dp')
- w_in_grad: float32 [4, 2048, 3072], P('pipe', 'dp')
- w_out_grad: float32 [4, 1024, 2048], P('pipe', 'dp')
Inputs may be any that keep to these rules, and one draw needn't show every extreme that they name: `segments`: in every row the history numbers run 0 to 3 without falling, each history has 1 to 64 positions, and one has exactly 64.
All inputs are finite; a program needn't handle non-finite values.
Results may differ from a plain program's by a relative error of at most 0.03.
Values may be sent and summed in bfloat16 or wider, within the bound.
A program may use at most 128 MiB of HBM per device.

v0:
```python
import jax
import jax.numpy as jnp
from jax import lax
from jax.sharding import PartitionSpec as P

HEADS = 16
QK_DIM = 32
V_DIM = 64
EPSILON = 1e-05


def passed_along(shard, axis, by):
    devices = lax.axis_size(axis)
    pairs = [(i, i + by) for i in range(devices) if 0 <= i + by < devices]
    return lax.ppermute(shard, axis, pairs)


def norm_rows(values):
    center = values - jnp.mean(values, axis=-1, keepdims=True)
    return center * lax.rsqrt(jnp.mean(center * center, axis=-1, keepdims=True) + EPSILON)


def silu_slope(preact):
    squash = jax.nn.sigmoid(preact)
    return squash * (1.0 + preact * (1.0 - squash))


def contract_rows(left, right):
    return lax.dot_general(
        left, right, (((0,), (0,)), ((), ())), preferred_element_type=jnp.float32
    )


def forward_front(inputs, w_first):
    normed = norm_rows(inputs.astype(jnp.float32)).astype(jnp.bfloat16)
    preact = jnp.dot(normed, w_first, preferred_element_type=jnp.float32)
    return (normed, preact, jax.nn.silu(preact).astype(jnp.bfloat16))


def attend(activated, history):
    row_count = activated.shape[0]
    value_cols = HEADS * V_DIM
    query_cols = HEADS * QK_DIM
    active32 = activated.astype(jnp.float32)
    gating = active32[:, :value_cols]
    values = active32[:, value_cols : 2 * value_cols].reshape(row_count, HEADS, V_DIM)
    queries = active32[:, 2 * value_cols : 2 * value_cols + query_cols].reshape(
        row_count, HEADS, QK_DIM
    )
    key_rows = active32[:, 2 * value_cols + query_cols :].reshape(row_count, HEADS, QK_DIM)
    scores = jnp.einsum("qhd,khd->hqk", queries, key_rows) * QK_DIM ** (-0.5)
    same_doc = history[:, None] == history[None, :]
    positions = lax.broadcasted_iota(jnp.int32, (row_count, row_count), 0)
    columns = lax.broadcasted_iota(jnp.int32, (row_count, row_count), 1)
    allowed = jnp.logical_and(same_doc, columns <= positions)
    counts = jnp.sum(same_doc.astype(jnp.float32), axis=1)
    weights_mask = allowed.astype(jnp.float32) / counts[:, None]
    weights = jax.nn.silu(scores) * weights_mask[None]
    mixed = jnp.einsum("hqk,khd->qhd", weights, values).reshape(row_count, value_cols)
    return norm_rows(mixed) * gating


def layer_back(inputs, preact, activated, upstream, history, w_first, w_second):
    gated_full, pull = jax.vjp(lambda active_in: attend(active_in, history), activated)
    gated = gated_full.astype(jnp.bfloat16)
    grad_second = contract_rows(gated, upstream)
    grad_gated = lax.dot_general(
        upstream, w_second, (((1,), (1,)), ((), ())), preferred_element_type=jnp.float32
    )
    (grad_active,) = pull(grad_gated)
    grad_preact = (grad_active.astype(jnp.float32) * silu_slope(preact)).astype(jnp.bfloat16)
    grad_normed = lax.dot_general(
        grad_preact, w_first, (((1,), (1,)), ((), ())), preferred_element_type=jnp.float32
    )
    _, pull_norm = jax.vjp(norm_rows, inputs.astype(jnp.float32))
    (grad_through,) = pull_norm(grad_normed)
    grad_input = (upstream.astype(jnp.float32) + grad_through).astype(jnp.bfloat16)
    return (grad_input, grad_preact, grad_second)


def body(section_input, top_grad, w_in, w_out, segments):
    w_first = lax.all_gather(w_in[0], "dp", axis=0, tiled=True)
    w_second = lax.all_gather(w_out[0], "dp", axis=0, tiled=True)
    sections = lax.axis_size("pipe")
    section = lax.axis_index("pipe")
    inputs_all = section_input[0]
    micro = segments.shape[0]
    length = segments.shape[1]
    width = inputs_all.shape[1]
    hidden_cols = w_first.shape[1]
    store = jnp.zeros((micro * length, hidden_cols), jnp.bfloat16)

    def one_step(step_index, carry):
        incoming, store_now, acc_out, grads = carry
        slot = step_index - (sections - 1 - section)
        active = jnp.logical_and(slot >= 0, slot < micro)
        slot = jnp.clip(slot, 0, micro - 1)
        start = slot * length
        top_rows = lax.dynamic_slice_in_dim(top_grad, start, length, 0)
        upstream = jnp.where(section == sections - 1, top_rows, incoming)
        history = lax.dynamic_index_in_dim(segments, slot, 0, keepdims=False)

        def work():
            inputs = lax.dynamic_slice_in_dim(inputs_all, start, length, 0)
            normed, preact, activated = forward_front(inputs, w_first)
            grad_input, grad_preact, grad_second = layer_back(
                inputs, preact, activated, upstream, history, w_first, w_second
            )
            store_next = lax.dynamic_update_slice_in_dim(store_now, grad_preact, start, 0)
            grads_next = lax.dynamic_update_slice_in_dim(grads, grad_input, start, 0)
            return (grad_input, store_next, acc_out + grad_second, grads_next)

        def resting():
            return (jnp.zeros_like(incoming), store_now, acc_out, grads)

        outgoing, store_now, acc_out, grads = lax.cond(active, work, resting)
        incoming = passed_along(outgoing, "pipe", -1)
        return (incoming, store_now, acc_out, grads)

    start_carry = (
        jnp.zeros((length, width), jnp.bfloat16),
        store,
        jnp.zeros((w_second.shape[0], width), jnp.float32),
        jnp.zeros_like(inputs_all),
    )
    _, store, acc_out, grads = lax.fori_loop(0, sections + micro - 1, one_step, start_carry)
    normed_rows = norm_rows(inputs_all.astype(jnp.float32)).astype(jnp.bfloat16)
    grad_first = lax.psum_scatter(
        contract_rows(normed_rows, store).astype(jnp.bfloat16),
        "dp",
        scatter_dimension=0,
        tiled=True,
    ).astype(jnp.float32)
    grad_out = lax.psum_scatter(
        acc_out.astype(jnp.bfloat16), "dp", scatter_dimension=0, tiled=True
    ).astype(jnp.float32)
    return (grads[None], grad_first[None], grad_out[None])


def solution(mesh):
    return jax.shard_map(
        body,
        mesh=mesh,
        in_specs=(
            P("pipe", "dp", None),
            P("dp", None),
            P("pipe", "dp", None),
            P("pipe", "dp", None),
            P("dp", None),
        ),
        out_specs=(P("pipe", "dp", None), P("pipe", "dp", None), P("pipe", "dp", None)),
        check_vma=False,
    )
```

profile of v0, /device:TPU:0, one launch (start us, length us, event | category | flops | bytes accessed | tf_op | source)
XLA Modules:
  0.0 868.3 jit_solution(9166335217495823203)
XLA Ops:
  8.7 76.9 %all-gather.5.cloned.1.call-done = bf16[1,1024,2048]{2,1,0:T(8,128)(2,1)} async-done(((bf16[1,128,2048]{2,1,0:T(8,128)(2,1)}), bf16[1,1024,2048]{2,1,0:T(8,128)(2,1)}) %all-gather.5.cloned.1.call-update) | async-done | bytes 4194320 | tf_op jit(solution)/shard_map/all_gather | solution.py:83
  85.6 176.9 %all-gather.7.cloned.1.call-done = bf16[1,2048,3072]{2,1,0:T(8,128)(2,1)} async-done(((bf16[1,256,3072]{2,1,0:T(8,128)(2,1)}), bf16[1,2048,3072]{2,1,0:T(8,128)(2,1)}) %all-gather.7.cloned.1.call-update) | async-done | bytes 12582928 | tf_op jit(solution)/shard_map/all_gather | solution.py:82
  264.7 4.3 broadcast_in_dim.57
  270.0 285.4 %while.21 = (s32[]{:T(128)}, bf16[128,2048]{1,0:T(8,128)(2,1)}, bf16[256,3072]{1,0:T(8,128)(2,1)}, f32[1024,2048]{1,0:T(8,128)}, bf16[256,2048]{1,0:T(8,128)(2,1...) while((s32[]{:T(128)}, bf16[128,2048]{1,0:T(8,128)(2,1)}, ...), condition=%wide.region_12.13_spmd, body=%wide.region_0.12_spmd.sunk | while | flops 4473488384 | bytes 157841232 | solution.py:126
  272.2 2.7 collective-permute-done
  277.8 8.8 %collective-permute-done = bf16[128,2048]{1,0:T(8,128)(2,1)S(1)} collective-permute-done((bf16[128,2048]{1,0:T(8,128)(2,1)}, bf16[128,2048]{1,0:T(8,128)(2,1)S(1)}, u32[]{:S(2)}, u32[]{:S(2)}) %collective-permute-start) | collective-permute-done | bytes 524320 | tf_op jit(solution)/shard_map/while/body/eval_jaxpr/ppermute | solution.py:15
  289.5 148.4 %collective-permute-done = bf16[128,2048]{1,0:T(8,128)(2,1)S(1)} collective-permute-done((bf16[128,2048]{1,0:T(8,128)(2,1)}, bf16[128,2048]{1,0:T(8,128)(2,1)S(1)}, u32[]{:S(2)}, u32[]{:S(2)}) %collective-permute-start) | collective-permute-done | bytes 524320 | tf_op jit(solution)/shard_map/while/body/eval_jaxpr/ppermute | solution.py:15
  438.8 50.1 %conditional.2 = (bf16[128,2048]{1,0:T(8,128)(2,1)}, bf16[256,3072]{1,0:T(8,128)(2,1)}, f32[1024,2048]{1,0:T(8,128)}, bf16[256,2048]{1,0:T(8,128)(2,1)}) conditional(s32[]{:T(128)} %convert_element_type.154, (bf16[256,3072]{1,0:T(8,128)(2,1)}, f32[1024,2048]{1,0:T(8,128)}, bf16[256,2048]{1,0:T(8,128)(2,1)}) %tuple.69, (pred[]{:T(512)}, s32[]{:T(128)}, ...), branch_computations={%region_1.1_spmd, %region_2.11_spmd} | conditional | flops 4473488384 | bytes 153646560 | solution.py:116
  439.3 7.9 multiply_convert_fusion.1
  451.2 3.8 multiply_reduce_fusion
  456.5 2.6 fusion.22
  460.4 2.1 fusion.9
  466.1 2.0 fusion.43
  469.9 3.2 constant_dynamic-update-slice_fusion
  473.1 9.0 %fusion.6 = (f32[128]{0:T(128)S(1)}, f32[128,2048]{1,0:T(8,128)S(1)}) fusion(f32[128]{0:T(128)S(1)} %broadcast_multiply_fusion.1, bf16[256,2048]{1,0:T(8,128)(2,1)S(1)} %get-tuple-element.374, s32[]{:T(128)S(6)} %select_n.43, bf16[128,3072]{1,0:T(8,128)(2,1)S(1)} %get-tuple-element.433, bf16[2048,3072]{1,0:T(8,128)(2,1)} %get-tuple-element.375), kind=kOutput, calls=%fused_computation.17 | convolution fusion | flops 1611661184 | bytes 14943236 | tf_op jit(solution)/shard_map/while/body/eval_jaxpr/cond/branch_1_fun/dot_general | solution.py:72
  485.7 3.2 copy-done
  490.2 9.4 %collective-permute-done = bf16[128,2048]{1,0:T(8,128)(2,1)S(1)} collective-permute-done((bf16[128,2048]{1,0:T(8,128)(2,1)}, bf16[128,2048]{1,0:T(8,128)(2,1)S(1)}, u32[]{:S(2)}, u32[]{:S(2)}) %collective-permute-start) | collective-permute-done | bytes 524320 | tf_op jit(solution)/shard_map/while/body/eval_jaxpr/ppermute | solution.py:15
  500.4 50.1 %conditional.2 = (bf16[128,2048]{1,0:T(8,128)(2,1)}, bf16[256,3072]{1,0:T(8,128)(2,1)}, f32[1024,2048]{1,0:T(8,128)}, bf16[256,2048]{1,0:T(8,128)(2,1)}) conditional(s32[]{:T(128)} %convert_element_type.154, (bf16[256,3072]{1,0:T(8,128)(2,1)}, f32[1024,2048]{1,0:T(8,128)}, bf16[256,2048]{1,0:T(8,128)(2,1)}) %tuple.69, (pred[]{:T(512)}, s32[]{:T(128)}, ...), branch_computations={%region_1.1_spmd, %region_2.11_spmd} | conditional | flops 4473488384 | bytes 153646560 | solution.py:116
  500.9 7.9 multiply_convert_fusion.1
  512.9 3.8 multiply_reduce_fusion
  518.2 2.6 fusion.22
  522.0 2.1 fusion.9
  531.5 3.2 constant_dynamic-update-slice_fusion
  534.8 9.0 %fusion.6 = (f32[128]{0:T(128)S(1)}, f32[128,2048]{1,0:T(8,128)S(1)}) fusion(f32[128]{0:T(128)S(1)} %broadcast_multiply_fusion.1, bf16[256,2048]{1,0:T(8,128)(2,1)S(1)} %get-tuple-element.374, s32[]{:T(128)S(6)} %select_n.43, bf16[128,3072]{1,0:T(8,128)(2,1)S(1)} %get-tuple-element.433, bf16[2048,3072]{1,0:T(8,128)(2,1)} %get-tuple-element.375), kind=kOutput, calls=%fused_computation.17 | convolution fusion | flops 1611661184 | bytes 14943236 | tf_op jit(solution)/shard_map/while/body/eval_jaxpr/cond/branch_1_fun/dot_general | solution.py:72
  547.4 3.2 copy-done
  551.9 2.7 collective-permute-done
  555.4 6.0 convert_element_type.89
  562.1 8.0 convolution_convert_fusion
  570.2 77.7 %reduce-scatter.5.cloned.1.call-done = bf16[128,2048]{1,0:T(8,128)(2,1)} async-done(((bf16[1024,2048]{1,0:T(8,128)(2,1)}), bf16[128,2048]{1,0:T(8,128)(2,1)}) %reduce-scatter.5.cloned.1.call-update) | async-done | bytes 524304 | tf_op jit(solution)/shard_map/reduce_scatter | solution.py:134
  647.9 2.1 bitcast_convert_fusion.1
  650.0 208.4 %reduce-scatter.3.cloned.1.call-done = bf16[256,3072]{1,0:T(8,128)(2,1)} async-done(((bf16[2048,3072]{1,0:T(8,128)(2,1)}), bf16[256,3072]{1,0:T(8,128)(2,1)}) %reduce-scatter.3.cloned.1.call-update) | async-done | bytes 1572880 | tf_op jit(solution)/shard_map/reduce_scatter | solution.py:128
  858.4 3.4 bitcast_convert_fusion
  (151 shorter events, 55.2 us)
Async XLA Ops:
  7.2 78.5 %all-gather.5.cloned.1.call-start = ((), (), s32[]{:S(2)}) async-start(), calls=%async_computation.4 | async-start | bytes 4718592 | tf_op jit(solution)/shard_map/all_gather | solution.py:83
  7.9 254.6 %all-gather.7.cloned.1.call-start = ((), (), s32[]{:S(2)}) async-start(), calls=%async_computation.5 | async-start | bytes 14155776 | tf_op jit(solution)/shard_map/all_gather | solution.py:82
  8.6 639.2 %reduce-scatter.5.cloned.1.call-start = ((), (), s32[]{:S(2)}) async-start(), calls=%async_computation.3 | async-start | bytes 4718592 | tf_op jit(solution)/shard_map/reduce_scatter | solution.py:134
  264.7 5.4 copy-start.1
  270.9 4.0 collective-permute-start
  276.5 10.1 %collective-permute-start = (bf16[128,2048]{1,0:T(8,128)(2,1)}, bf16[128,2048]{1,0:T(8,128)(2,1)S(1)}, u32[]{:S(2)}, u32[]{:S(2)}) collective-permute-start(bf16[128,2048]{1,0:T(8,128)(2,1)} %get-tuple-element.526), channel_id=1, source_target_pairs={{8,0},{16,8},{24,16},{9,1},{17,9},{25,17},{10,2},{18,10},{26,18},{... | collective-permute-start | bytes 1572872 | tf_op jit(solution)/shard_map/while/body/eval_jaxpr/ppermute | solution.py:15
  286.6 0.8 copy-start.6
  288.3 149.7 %collective-permute-start = (bf16[128,2048]{1,0:T(8,128)(2,1)}, bf16[128,2048]{1,0:T(8,128)(2,1)S(1)}, u32[]{:S(2)}, u32[]{:S(2)}) collective-permute-start(bf16[128,2048]{1,0:T(8,128)(2,1)} %get-tuple-element.526), channel_id=1, source_target_pairs={{8,0},{16,8},{24,16},{9,1},{17,9},{25,17},{10,2},{18,10},{26,18},{... | collective-permute-start | bytes 1572872 | tf_op jit(solution)/shard_map/while/body/eval_jaxpr/ppermute | solution.py:15
  439.2 7.9 copy-start.10
  447.3 2.2 copy-start.7
  447.6 1.9 copy-start.3
  448.0 1.6 copy-start.5
  456.5 2.6 copy-start.8
  460.3 2.9 copy-start.4
  469.9 14.1 %slice-start = ((s8[8388608]{0:T(1024)(128)(4,1)}), s8[4194304]{0:T(1024)(128)(4,1)S(1)}, s32[]{:S(2)}) async-start(s8[8388608]{0:T(1024)(128)(4,1)} %bitcast.58), calls=%async_computation.6 | async-start | bytes 8388608 | tf_op jit(solution)/shard_map/while/body/eval_jaxpr/cond
  473.1 9.0 %copy-start.11 = (f32[128]{0:T(128)S(1)}, f32[128]{0:T(128)}, u32[]{:S(2)}) copy-start(f32[128]{0:T(128)} %copy-done.10) | copy-start | bytes 1540 | tf_op jit(solution)/shard_map/while/body/eval_jaxpr/cond
  473.1 10.9 %slice-start.1 = ((s8[8388608]{0:T(1024)(128)(4,1)}), s8[4194304]{0:T(1024)(128)(4,1)S(1)}, s32[]{:S(2)}) async-start(s8[8388608]{0:T(1024)(128)(4,1)} %bitcast.58), calls=%async_computation.7 | async-start | bytes 8388608 | tf_op jit(solution)/shard_map/while/body/eval_jaxpr/cond
  485.7 3.2 copy-start
  488.9 10.7 %collective-permute-start = (bf16[128,2048]{1,0:T(8,128)(2,1)}, bf16[128,2048]{1,0:T(8,128)(2,1)S(1)}, u32[]{:S(2)}, u32[]{:S(2)}) collective-permute-start(bf16[128,2048]{1,0:T(8,128)(2,1)} %get-tuple-element.526), channel_id=1, source_target_pairs={{8,0},{16,8},{24,16},{9,1},{17,9},{25,17},{10,2},{18,10},{26,18},{... | collective-permute-start | bytes 1572872 | tf_op jit(solution)/shard_map/while/body/eval_jaxpr/ppermute | solution.py:15
  499.6 0.8 copy-start.6
  500.9 7.9 copy-start.10
  509.0 2.2 copy-start.7
  509.3 1.9 copy-start.3
  509.6 1.6 copy-start.5
  518.1 2.6 copy-start.8
  522.0 2.9 copy-start.4
  531.5 14.1 %slice-start = ((s8[8388608]{0:T(1024)(128)(4,1)}), s8[4194304]{0:T(1024)(128)(4,1)S(1)}, s32[]{:S(2)}) async-start(s8[8388608]{0:T(1024)(128)(4,1)} %bitcast.58), calls=%async_computation.6 | async-start | bytes 8388608 | tf_op jit(solution)/shard_map/while/body/eval_jaxpr/cond
  534.8 9.0 %copy-start.11 = (f32[128]{0:T(128)S(1)}, f32[128]{0:T(128)}, u32[]{:S(2)}) copy-start(f32[128]{0:T(128)} %copy-done.10) | copy-start | bytes 1540 | tf_op jit(solution)/shard_map/while/body/eval_jaxpr/cond
  534.8 10.9 %slice-start.1 = ((s8[8388608]{0:T(1024)(128)(4,1)}), s8[4194304]{0:T(1024)(128)(4,1)S(1)}, s32[]{:S(2)}) async-start(s8[8388608]{0:T(1024)(128)(4,1)} %bitcast.58), calls=%async_computation.7 | async-start | bytes 8388608 | tf_op jit(solution)/shard_map/while/body/eval_jaxpr/cond
  547.4 3.2 copy-start
  550.6 4.0 collective-permute-start
  561.4 296.9 %reduce-scatter.3.cloned.1.call-start = ((), (), s32[]{:S(2)}) async-start(), calls=%async_computation.2 | async-start | bytes 14155776 | tf_op jit(solution)/shard_map/reduce_scatter | solution.py:128
  (7 other events, 5.3 us)
Sparse Core Ops, SparseCore 0:
  10.1 75.5 all-gather.4
  87.8 174.6 all-gather.6
  561.5 86.2 reduce-scatter.4
  651.3 207.0 reduce-scatter.2
where the time goes:
time: 869 us; the launch traced here: 868 us
  waiting for transfers between devices  713 us (82%)
  matrix products  70 us (8%)
  local copies, waits for them, and re-layouts  35.1 us (4%)
  other arithmetic  29.1 us (3%)
  between operations  13.8 us (2%)
    reduce_scatter x1, waiting for transfers between devices, body(): lax.psum_scatter(contract_rows(normed_rows, store).astype(jnp.bfloat16),...  208 us
    all_gather x1, waiting for transfers between devices, body(): w_first = lax.all_gather(w_in[0], 'dp', axis=0, tiled=True)  177 us
    ppermute x5, waiting for transfers between devices, passed_along(): return lax.ppermute(shard, axis, pairs)  172 us
    reduce_scatter x1, waiting for transfers between devices, body(): lax.psum_scatter(acc_out.astype(jnp.bfloat16), 'dp', scatter_dimension=0,...  77.7 us
    all_gather x1, waiting for transfers between devices, body(): w_second = lax.all_gather(w_out[0], 'dp', axis=0, tiled=True)  76.9 us
    dot_general x2, matrix products, layer_back(): lax.dot_general(grad_preact, w_first, (((1,), (1,)), ((), ())), preferred...  18.1 us
  transfers between devices with their start and end apart: 9, of which 9 were waited for; matrix products, arithmetic and copies ran while one was open for 1% of the time, Pallas kernels for 0%

commit v1 on v0

--- a/solution.py
+++ b/solution.py
@@ -1,3 +1,4 @@
+import functools
 import jax
 import jax.numpy as jnp
 from jax import lax
@@ -7,6 +8,34 @@
 QK_DIM = 32
 V_DIM = 64
 EPSILON = 1e-05
+
+
+def drive_loops(mine, mesh_name):
+    frame_out = jax.lax.axis_index(mesh_name)
+    block_out = jax.lax.axis_size(mesh_name)
+    front, piece_now, arr_out = (block_out, frame_out, mine.shape[0])
+    fields = [m * front if nth == 0 else m for nth, m in enumerate(mine.shape)]
+    tile_out = jnp.zeros(fields, mine.dtype)
+    side_arr = lax.dynamic_update_slice_in_dim(tile_out, mine, piece_now * arr_out, axis=0)
+    mixed_arr = current_arr = mine
+    for pp in range(1, front // 2 + 1):
+        mixed_arr = jax.lax.ppermute(
+            mixed_arr, mesh_name, list(map(lambda nth: (nth, (nth + 1) % front), range(front)))
+        )
+        side_arr = lax.dynamic_update_slice_in_dim(
+            side_arr, mixed_arr, (piece_now - pp) % front * arr_out, axis=0
+        )
+        if 2 * pp < front:
+            p_next = map(lambda nth: (nth, (nth - 1) % front), range(front))
+            small = list(p_next)
+            current_arr = jax.lax.ppermute(current_arr, mesh_name, small)
+            side_arr = lax.dynamic_update_slice_in_dim(
+                side_arr, current_arr, (piece_now + pp) % front * arr_out, axis=0
+            )
+    return side_arr
+
+
+plan_packet_up = functools.partial(drive_loops, mesh_name="dp")
 
 
 def passed_along(shard, axis, by):
@@ -80,7 +109,7 @@
 
 def body(section_input, top_grad, w_in, w_out, segments):
     w_first = lax.all_gather(w_in[0], "dp", axis=0, tiled=True)
-    w_second = lax.all_gather(w_out[0], "dp", axis=0, tiled=True)
+    w_second = plan_packet_up(w_out[0])
     sections = lax.axis_size("pipe")
     section = lax.axis_index("pipe")
     inputs_all = section_input[0]

time: 869 us -> 830 us (0.955)
  waiting for transfers between devices: 713 us -> 648 us
  starting transfers between devices: 6.55 us -> 22.6 us
  local copies, waits for them, and re-layouts: 35.1 us -> 44.4 us
    ppermute x0 -> x7, waiting for transfers between devices: none -> 89.4 us  [the longest x4 88.2 us: drive_loops(): jax.lax.ppermute(mixed_arr, mesh_name, list(map(lambda nth: (nth, (nth +...]
    all_gather x1 -> x0, waiting for transfers between devices: 76.9 us -> none  [body(): w_second = lax.all_gather(w_out[0], 'dp', axis=0, tiled=True)]
    all_gather x1, waiting for transfers between devices: 177 us -> 101 us  [body(): w_first = lax.all_gather(w_in[0], 'dp', axis=0, tiled=True)]
    ppermute x0 -> x7, starting transfers between devices: none -> 16 us  [the longest x3 8.13 us: drive_loops(): current_arr = jax.lax.ppermute(current_arr, mesh_name, small)]
  transfers between devices with their start and end apart: 9 -> 15, of which waited for: 9 -> 13; matrix products, arithmetic and copies ran while one was open for 1% -> 2% of each run, Pallas kernels for 0% -> 0%
where the time goes in v1:
time: 830 us; the launch traced here: 828 us
  waiting for transfers between devices  648 us (78%)
  matrix products  70 us (8%)
  local copies, waits for them, and re-layouts  44.4 us (5%)
  other arithmetic  28.8 us (3%)
  starting transfers between devices  22.6 us (3%)
  between operations  13.8 us (2%)
    reduce_scatter x1, waiting for transfers between devices, body(): lax.psum_scatter(contract_rows(normed_rows, store).astype(jnp.bfloat16),...  209 us
    ppermute x5, waiting for transfers between devices, passed_along(): return lax.ppermute(shard, axis, pairs)  172 us
    all_gather x1, waiting for transfers between devices, body(): w_first = lax.all_gather(w_in[0], 'dp', axis=0, tiled=True)  101 us
    ppermute x4, waiting for transfers between devices, drive_loops(): jax.lax.ppermute(mixed_arr, mesh_name, list(map(lambda nth: (nth, (nth +...  88.2 us
    reduce_scatter x1, waiting for transfers between devices, body(): lax.psum_scatter(acc_out.astype(jnp.bfloat16), 'dp', scatter_dimension=0,...  77.3 us
    dot_general x2, matrix products, layer_back(): lax.dot_general(grad_preact, w_first, (((1,), (1,)), ((), ())), preferred...  18.1 us
  transfers between devices with their start and end apart: 15, of which 13 were waited for; matrix products, arithmetic and copies ran while one was open for 2% of the time, Pallas kernels for 0%

profile of v1, /device:TPU:0, one launch (start us, length us, event | category | flops | bytes accessed | tf_op | source)
XLA Modules:
  0.0 828.5 jit_solution(17890933168850872709)
XLA Ops:
  7.9 3.0 collective-permute-start.1
  11.0 3.1 collective-permute-start.2
  14.1 29.9 %collective-permute-done.1 = bf16[128,2048]{1,0:T(8,128)(2,1)S(1)} collective-permute-done((bf16[128,2048]{1,0:T(8,128)(2,1)}, bf16[128,2048]{1,0:T(8,128)(2,1)S(1)}, u32[]{:S(2)}, u32[]{:S(2)}) %collective-permute-start.1) | collective-permute-done | bytes 524320 | tf_op jit(solution)/shard_map/ppermute | solution.py:22
  53.1 19.9 %collective-permute-done.3 = bf16[128,2048]{1,0:T(8,128)(2,1)S(1)} collective-permute-done((bf16[128,2048]{1,0:T(8,128)(2,1)S(1)}, bf16[128,2048]{1,0:T(8,128)(2,1)S(1)}, u32[]{:S(2)}, u32[]{:S(2)}) %collective-permute-start.3) | collective-permute-done | bytes 524320 | tf_op jit(solution)/shard_map/ppermute | solution.py:22
  77.2 3.0 collective-permute-start.6
  81.0 20.9 %collective-permute-done.5 = bf16[128,2048]{1,0:T(8,128)(2,1)S(1)} collective-permute-done((bf16[128,2048]{1,0:T(8,128)(2,1)S(1)}, bf16[128,2048]{1,0:T(8,128)(2,1)S(1)}, u32[]{:S(2)}, u32[]{:S(2)}) %collective-permute-start.5) | collective-permute-done | bytes 524320 | tf_op jit(solution)/shard_map/ppermute | solution.py:22
  104.4 17.4 %collective-permute-done.7 = bf16[128,2048]{1,0:T(8,128)(2,1)S(1)} collective-permute-done((bf16[128,2048]{1,0:T(8,128)(2,1)S(1)}, bf16[128,2048]{1,0:T(8,128)(2,1)S(1)}, u32[]{:S(2)}, u32[]{:S(2)}) %collective-permute-start.7) | collective-permute-done | bytes 524320 | tf_op jit(solution)/shard_map/ppermute | solution.py:22
  122.7 100.6 %all-gather.3.cloned.1.call-done = bf16[1,2048,3072]{2,1,0:T(8,128)(2,1)} async-done(((bf16[1,256,3072]{2,1,0:T(8,128)(2,1)}), bf16[1,2048,3072]{2,1,0:T(8,128)(2,1)}) %all-gather.3.cloned.1.call-update) | async-done | bytes 12582928 | tf_op jit(solution)/shard_map/all_gather | solution.py:111
  225.5 4.3 broadcast_in_dim.60
  230.8 284.9 %while.21 = (s32[]{:T(128)}, bf16[128,2048]{1,0:T(8,128)(2,1)}, bf16[256,3072]{1,0:T(8,128)(2,1)}, f32[1024,2048]{1,0:T(8,128)}, bf16[256,2048]{1,0:T(8,128)(2,1...) while((s32[]{:T(128)}, bf16[128,2048]{1,0:T(8,128)(2,1)}, ...), condition=%wide.region_12.13_spmd, body=%wide.region_0.12_spmd.sunk | while | flops 4473488384 | bytes 157841232 | solution.py:155
  233.0 2.7 collective-permute-done
  238.6 8.8 %collective-permute-done = bf16[128,2048]{1,0:T(8,128)(2,1)S(1)} collective-permute-done((bf16[128,2048]{1,0:T(8,128)(2,1)}, bf16[128,2048]{1,0:T(8,128)(2,1)S(1)}, u32[]{:S(2)}, u32[]{:S(2)}) %collective-permute-start) | collective-permute-done | bytes 524320 | tf_op jit(solution)/shard_map/while/body/eval_jaxpr/ppermute | solution.py:44
  250.4 148.2 %collective-permute-done = bf16[128,2048]{1,0:T(8,128)(2,1)S(1)} collective-permute-done((bf16[128,2048]{1,0:T(8,128)(2,1)}, bf16[128,2048]{1,0:T(8,128)(2,1)S(1)}, u32[]{:S(2)}, u32[]{:S(2)}) %collective-permute-start) | collective-permute-done | bytes 524320 | tf_op jit(solution)/shard_map/while/body/eval_jaxpr/ppermute | solution.py:44
  399.4 50.0 %conditional.2 = (bf16[128,2048]{1,0:T(8,128)(2,1)}, bf16[256,3072]{1,0:T(8,128)(2,1)}, f32[1024,2048]{1,0:T(8,128)}, bf16[256,2048]{1,0:T(8,128)(2,1)}) conditional(s32[]{:T(128)} %convert_element_type.154, (bf16[256,3072]{1,0:T(8,128)(2,1)}, f32[1024,2048]{1,0:T(8,128)}, bf16[256,2048]{1,0:T(8,128)(2,1)}) %tuple.69, (pred[]{:T(512)}, s32[]{:T(128)}, ...), branch_computations={%region_1.1_spmd, %region_2.11_spmd} | conditional | flops 4473488384 | bytes 153646560 | solution.py:145
  399.9 7.9 multiply_convert_fusion.1
  411.8 3.8 multiply_reduce_fusion
  430.5 3.1 constant_dynamic-update-slice_fusion
  433.6 9.0 %fusion.6 = (f32[128]{0:T(128)S(1)}, f32[128,2048]{1,0:T(8,128)S(1)}) fusion(f32[128]{0:T(128)S(1)} %broadcast_multiply_fusion.1, bf16[256,2048]{1,0:T(8,128)(2,1)S(1)} %get-tuple-element.374, s32[]{:T(128)S(6)} %select_n.83, bf16[128,3072]{1,0:T(8,128)(2,1)S(1)} %get-tuple-element.433, bf16[2048,3072]{1,0:T(8,128)(2,1)} %get-tuple-element.375), kind=kOutput, calls=%fused_computation.17 | convolution fusion | flops 1611661184 | bytes 14943236 | tf_op jit(solution)/shard_map/while/body/eval_jaxpr/cond/branch_1_fun/dot_general | solution.py:101
  446.2 3.2 copy-done
  450.7 9.4 %collective-permute-done = bf16[128,2048]{1,0:T(8,128)(2,1)S(1)} collective-permute-done((bf16[128,2048]{1,0:T(8,128)(2,1)}, bf16[128,2048]{1,0:T(8,128)(2,1)S(1)}, u32[]{:S(2)}, u32[]{:S(2)}) %collective-permute-start) | collective-permute-done | bytes 524320 | tf_op jit(solution)/shard_map/while/body/eval_jaxpr/ppermute | solution.py:44
  460.9 50.0 %conditional.2 = (bf16[128,2048]{1,0:T(8,128)(2,1)}, bf16[256,3072]{1,0:T(8,128)(2,1)}, f32[1024,2048]{1,0:T(8,128)}, bf16[256,2048]{1,0:T(8,128)(2,1)}) conditional(s32[]{:T(128)} %convert_element_type.154, (bf16[256,3072]{1,0:T(8,128)(2,1)}, f32[1024,2048]{1,0:T(8,128)}, bf16[256,2048]{1,0:T(8,128)(2,1)}) %tuple.69, (pred[]{:T(512)}, s32[]{:T(128)}, ...), branch_computations={%region_1.1_spmd, %region_2.11_spmd} | conditional | flops 4473488384 | bytes 153646560 | solution.py:145
  461.4 7.9 multiply_convert_fusion.1
  473.3 3.8 multiply_reduce_fusion
  492.0 3.1 constant_dynamic-update-slice_fusion
  495.1 9.0 %fusion.6 = (f32[128]{0:T(128)S(1)}, f32[128,2048]{1,0:T(8,128)S(1)}) fusion(f32[128]{0:T(128)S(1)} %broadcast_multiply_fusion.1, bf16[256,2048]{1,0:T(8,128)(2,1)S(1)} %get-tuple-element.374, s32[]{:T(128)S(6)} %select_n.83, bf16[128,3072]{1,0:T(8,128)(2,1)S(1)} %get-tuple-element.433, bf16[2048,3072]{1,0:T(8,128)(2,1)} %get-tuple-element.375), kind=kOutput, calls=%fused_computation.17 | convolution fusion | flops 1611661184 | bytes 14943236 | tf_op jit(solution)/shard_map/while/body/eval_jaxpr/cond/branch_1_fun/dot_general | solution.py:101
  507.7 3.2 copy-done
  512.2 2.7 collective-permute-done
  515.8 6.0 convert_element_type.89
  522.5 8.0 convolution_convert_fusion
  530.5 77.3 %reduce-scatter.5.cloned.1.call-done = bf16[128,2048]{1,0:T(8,128)(2,1)} async-done(((bf16[1024,2048]{1,0:T(8,128)(2,1)}), bf16[128,2048]{1,0:T(8,128)(2,1)}) %reduce-scatter.5.cloned.1.call-update) | async-done | bytes 524304 | tf_op jit(solution)/shard_map/reduce_scatter | solution.py:163
  610.0 208.6 %reduce-scatter.3.cloned.1.call-done = bf16[256,3072]{1,0:T(8,128)(2,1)} async-done(((bf16[2048,3072]{1,0:T(8,128)(2,1)}), bf16[256,3072]{1,0:T(8,128)(2,1)}) %reduce-scatter.3.cloned.1.call-update) | async-done | bytes 1572880 | tf_op jit(solution)/shard_map/reduce_scatter | solution.py:157
  818.5 3.4 bitcast_convert_fusion
  (173 shorter events, 85.5 us)
Async XLA Ops:
  7.2 216.1 %all-gather.3.cloned.1.call-start = ((), (), s32[]{:S(2)}) async-start(), calls=%async_computation.4 | async-start | bytes 14155776 | tf_op jit(solution)/shard_map/all_gather | solution.py:111
  7.9 599.9 %reduce-scatter.5.cloned.1.call-start = ((), (), s32[]{:S(2)}) async-start(), calls=%async_computation.3 | async-start | bytes 4718592 | tf_op jit(solution)/shard_map/reduce_scatter | solution.py:163
  7.9 36.1 %collective-permute-start.1 = (bf16[128,2048]{1,0:T(8,128)(2,1)}, bf16[128,2048]{1,0:T(8,128)(2,1)S(1)}, u32[]{:S(2)}, u32[]{:S(2)}) collective-permute-start(bf16[128,2048]{1,0:T(8,128)(2,1)} %bitcast.78), channel_id=1, source_target_pairs={{0,1},{1,2},{2,3},{3,4},{4,5},{5,6},{6,7},{7,0},{8,9},{9,10},{10,1... | collective-permute-start | bytes 1572872 | tf_op jit(solution)/shard_map/ppermute | solution.py:22
  11.0 36.7 %collective-permute-start.2 = (bf16[128,2048]{1,0:T(8,128)(2,1)}, bf16[128,2048]{1,0:T(8,128)(2,1)S(1)}, u32[]{:S(2)}, u32[]{:S(2)}) collective-permute-start(bf16[128,2048]{1,0:T(8,128)(2,1)} %bitcast.79), channel_id=1, source_target_pairs={{0,7},{1,0},{2,1},{3,2},{4,3},{5,4},{6,5},{7,6},{8,15},{9,8},{10,9... | collective-permute-start | bytes 1572872 | tf_op jit(solution)/shard_map/ppermute | solution.py:31
  44.0 28.9 %collective-permute-start.3 = (bf16[128,2048]{1,0:T(8,128)(2,1)S(1)}, bf16[128,2048]{1,0:T(8,128)(2,1)S(1)}, u32[]{:S(2)}, u32[]{:S(2)}) collective-permute-start(bf16[128,2048]{1,0:T(8,128)(2,1)S(1)} %collective-permute-done.1), channel_id=1, source_target_pairs={{0,1},{1,2},{2,3},{3,4},{4,5},{5,6},{6,7},{7,0},{8,9},{9,10},{10,1... | collective-permute-start | bytes 1572872 | tf_op jit(solution)/shard_map/ppermute | solution.py:22
  46.4 5.8 copy-start.10
  47.7 29.5 %collective-permute-start.4 = (bf16[128,2048]{1,0:T(8,128)(2,1)S(1)}, bf16[128,2048]{1,0:T(8,128)(2,1)S(1)}, u32[]{:S(2)}, u32[]{:S(2)}) collective-permute-start(bf16[128,2048]{1,0:T(8,128)(2,1)S(1)} %collective-permute-done.2), channel_id=1, source_target_pairs={{0,7},{1,0},{2,1},{3,2},{4,3},{5,4},{6,5},{7,6},{8,15},{9,8},{10,9... | collective-permute-start | bytes 1572872 | tf_op jit(solution)/shard_map/ppermute | solution.py:31
  72.9 29.0 %collective-permute-start.5 = (bf16[128,2048]{1,0:T(8,128)(2,1)S(1)}, bf16[128,2048]{1,0:T(8,128)(2,1)S(1)}, u32[]{:S(2)}, u32[]{:S(2)}) collective-permute-start(bf16[128,2048]{1,0:T(8,128)(2,1)S(1)} %collective-permute-done.3), channel_id=1, source_target_pairs={{0,1},{1,2},{2,3},{3,4},{4,5},{5,6},{6,7},{7,0},{8,9},{9,10},{10,1... | collective-permute-start | bytes 1572872 | tf_op jit(solution)/shard_map/ppermute | solution.py:22
  77.2 26.5 %collective-permute-start.6 = (bf16[128,2048]{1,0:T(8,128)(2,1)S(1)}, bf16[128,2048]{1,0:T(8,128)(2,1)S(1)}, u32[]{:S(2)}, u32[]{:S(2)}) collective-permute-start(bf16[128,2048]{1,0:T(8,128)(2,1)S(1)} %collective-permute-done.4), channel_id=1, source_target_pairs={{0,7},{1,0},{2,1},{3,2},{4,3},{5,4},{6,5},{7,6},{8,15},{9,8},{10,9... | collective-permute-start | bytes 1572872 | tf_op jit(solution)/shard_map/ppermute | solution.py:31
  101.9 19.9 %collective-permute-start.7 = (bf16[128,2048]{1,0:T(8,128)(2,1)S(1)}, bf16[128,2048]{1,0:T(8,128)(2,1)S(1)}, u32[]{:S(2)}, u32[]{:S(2)}) collective-permute-start(bf16[128,2048]{1,0:T(8,128)(2,1)S(1)} %collective-permute-done.5), channel_id=1, source_target_pairs={{0,1},{1,2},{2,3},{3,4},{4,5},{5,6},{6,7},{7,0},{8,9},{9,10},{10,1... | collective-permute-start | bytes 1572872 | tf_op jit(solution)/shard_map/ppermute | solution.py:22
  225.5 5.3 copy-start.1
  231.7 4.0 collective-permute-start
  237.3 10.1 %collective-permute-start = (bf16[128,2048]{1,0:T(8,128)(2,1)}, bf16[128,2048]{1,0:T(8,128)(2,1)S(1)}, u32[]{:S(2)}, u32[]{:S(2)}) collective-permute-start(bf16[128,2048]{1,0:T(8,128)(2,1)} %get-tuple-element.526), channel_id=1, source_target_pairs={{8,0},{16,8},{24,16},{9,1},{17,9},{25,17},{10,2},{18,10},{26,18},{... | collective-permute-start | bytes 1572872 | tf_op jit(solution)/shard_map/while/body/eval_jaxpr/ppermute | solution.py:44
  249.1 149.5 %collective-permute-start = (bf16[128,2048]{1,0:T(8,128)(2,1)}, bf16[128,2048]{1,0:T(8,128)(2,1)S(1)}, u32[]{:S(2)}, u32[]{:S(2)}) collective-permute-start(bf16[128,2048]{1,0:T(8,128)(2,1)} %get-tuple-element.526), channel_id=1, source_target_pairs={{8,0},{16,8},{24,16},{9,1},{17,9},{25,17},{10,2},{18,10},{26,18},{... | collective-permute-start | bytes 1572872 | tf_op jit(solution)/shard_map/while/body/eval_jaxpr/ppermute | solution.py:44
  399.8 7.9 copy-start.11
  417.1 2.6 copy-start.8
  420.9 2.9 copy-start.4
  433.6 10.9 %slice-start = ((s8[8388608]{0:T(1024)(128)(4,1)}), s8[4194304]{0:T(1024)(128)(4,1)S(1)}, s32[]{:S(2)}) async-start(s8[8388608]{0:T(1024)(128)(4,1)} %bitcast.59), calls=%async_computation.5 | async-start | bytes 8388608 | tf_op jit(solution)/shard_map/while/body/eval_jaxpr/cond
  433.6 9.0 %copy-start.12 = (f32[128]{0:T(128)S(1)}, f32[128]{0:T(128)}, u32[]{:S(2)}) copy-start(f32[128]{0:T(128)} %copy-done.11) | copy-start | bytes 1540 | tf_op jit(solution)/shard_map/while/body/eval_jaxpr/cond
  433.6 10.9 %slice-start.1 = ((s8[8388608]{0:T(1024)(128)(4,1)}), s8[4194304]{0:T(1024)(128)(4,1)S(1)}, s32[]{:S(2)}) async-start(s8[8388608]{0:T(1024)(128)(4,1)} %bitcast.59), calls=%async_computation.6 | async-start | bytes 8388608 | tf_op jit(solution)/shard_map/while/body/eval_jaxpr/cond
  446.2 3.2 copy-start
  449.4 10.7 %collective-permute-start = (bf16[128,2048]{1,0:T(8,128)(2,1)}, bf16[128,2048]{1,0:T(8,128)(2,1)S(1)}, u32[]{:S(2)}, u32[]{:S(2)}) collective-permute-start(bf16[128,2048]{1,0:T(8,128)(2,1)} %get-tuple-element.526), channel_id=1, source_target_pairs={{8,0},{16,8},{24,16},{9,1},{17,9},{25,17},{10,2},{18,10},{26,18},{... | collective-permute-start | bytes 1572872 | tf_op jit(solution)/shard_map/while/body/eval_jaxpr/ppermute | solution.py:44
  461.4 7.9 copy-start.11
  469.4 2.2 copy-start.7
  478.6 2.6 copy-start.8
  482.5 2.9 copy-start.4
  495.1 10.9 %slice-start = ((s8[8388608]{0:T(1024)(128)(4,1)}), s8[4194304]{0:T(1024)(128)(4,1)S(1)}, s32[]{:S(2)}) async-start(s8[8388608]{0:T(1024)(128)(4,1)} %bitcast.59), calls=%async_computation.5 | async-start | bytes 8388608 | tf_op jit(solution)/shard_map/while/body/eval_jaxpr/cond
  495.1 9.0 %copy-start.12 = (f32[128]{0:T(128)S(1)}, f32[128]{0:T(128)}, u32[]{:S(2)}) copy-start(f32[128]{0:T(128)} %copy-done.11) | copy-start | bytes 1540 | tf_op jit(solution)/shard_map/while/body/eval_jaxpr/cond
  495.1 10.9 %slice-start.1 = ((s8[8388608]{0:T(1024)(128)(4,1)}), s8[4194304]{0:T(1024)(128)(4,1)S(1)}, s32[]{:S(2)}) async-start(s8[8388608]{0:T(1024)(128)(4,1)} %bitcast.59), calls=%async_computation.6 | async-start | bytes 8388608 | tf_op jit(solution)/shard_map/while/body/eval_jaxpr/cond
  507.7 3.2 copy-start
  510.9 4.0 collective-permute-start
  521.8 296.7 %reduce-scatter.3.cloned.1.call-start = ((), (), s32[]{:S(2)}) async-start(), calls=%async_computation.2 | async-start | bytes 14155776 | tf_op jit(solution)/shard_map/reduce_scatter | solution.py:157
  (14 other events, 16.1 us)
Sparse Core Ops, SparseCore 0:
  10.2 213.0 all-gather.2
  521.9 85.8 reduce-scatter.4
  611.4 207.0 reduce-scatter.2
